TPU v7x, 512 devices: a whole 4x8x8 slice. The times are simulated.
512 devices in a mesh: req: 128 (over z, y, core), mlp: 4 (over x).
Axes of the slice: x: 4, y: 8, z: 8, core: 2. Of those that a mesh axis runs over, the one named last changes fastest.
Arguments:
- patches: bfloat16 [16384, 4, 1280], P('req', 'mlp'), may hold values from -6 to 6
- vis_gain: float32 [1280], replicated, may hold values from 0.5 to 1.5
- proj_weight: bfloat16 [4, 1280, 1280], P('mlp', 'req'), may hold values from -0.078125 to 0.078125
- image_dest: int32 [16384, 1], P('req'), may hold values from 0 to 127; in each aligned block of 128 rows (0 to 127, 128 to 255, ...) at most 2 rows name the same one
- image_pos: int32 [128], P('req'), may hold values from 0 to 255
- text_len: int32 [128], P('req'), may hold values from 64 to 255
- text: bfloat16 [128, 256, 1280], P('req'), may hold values from -6 to 6
- attn_gain: float32 [1280], replicated, may hold values from 0.5 to 1.5
- qkv_weight: bfloat16 [3, 1280, 1280], P(None, 'req', 'mlp'), may hold values from -0.15625 to 0.15625
- out_weight: bfloat16 [1280, 1280], P('mlp', 'req'), may hold values from -0.15625 to 0.15625
- cache_keys: bfloat16 [128, 1280, 1280], P('req', None, 'mlp')
- cache_values: bfloat16 [128, 1280, 1280], P('req', None, 'mlp'), may hold values from -6 to 6
- held: bfloat16 [16384, 1280], P('req'), may hold values from -6 to 6
- held_owner: int32 [128, 128, 1], P('req'), may hold values from 0 to 127; in each aligned block of 128 rows (0 to 127, 128 to 255, ..., all dimensions but the last counted through in order) at most 2 rows name the same one
- held_row: int32 [128, 128], P('req'), may hold values from 0 to 127
- recompute_pos: int32 [128, 128], P('req'), may hold values from 0 to 1279, as said below
Outputs:
- attended: bfloat16 [128, 256, 1280], P('req', None, 'mlp')
Inputs may be any that keep to these rules, and one draw needn't show every extreme that they name: `image_dest`: within each aligned block of 128 rows no request is named more than 2 times. `held_owner`: within each request's 128 rows no owner is named more than 2 times. `recompute_pos`: the positions of one request are distinct.
All inputs are finite; a program needn't handle non-finite values.
Results may differ from a plain program's by a relative error of at most 0.013.
The roundings to bfloat16 on the way count: a program that leaves them out, or rounds other values in their place, can miss the bound.
Values may be sent and summed in bfloat16 or wider, within the bound.
A program may use at most 128 MiB of HBM per device.

v0:
```python
import jax
import jax.numpy as jnp
from jax import lax
from jax.sharding import PartitionSpec as P

HEAD_DIM = 80
eps = 1e-06
big_negative = -1e30


def norm_rows(values, gain):
    floats = values.astype(jnp.float32)
    return (floats * lax.rsqrt(jnp.mean(floats * floats, -1, keepdims=True) + eps) * gain).astype(
        jnp.bfloat16
    )


def attend(queries, all_keys, all_values, length):
    seq_len = queries.shape[0]
    cache_len = all_keys.shape[0] - seq_len
    head_count = queries.shape[1] // HEAD_DIM
    query_heads = queries.reshape(seq_len, head_count, HEAD_DIM)
    key_heads = all_keys.reshape(-1, head_count, HEAD_DIM)
    value_heads = all_values.reshape(-1, head_count, HEAD_DIM)
    scores = jnp.einsum(
        "qhd,khd->hqk", query_heads, key_heads, preferred_element_type=jnp.float32
    ) * HEAD_DIM ** (-0.5)
    row_ids = jnp.arange(seq_len, dtype=jnp.int32)[:, None]
    col_ids = jnp.arange(all_keys.shape[0], dtype=jnp.int32)[None, :] - cache_len
    allowed = (col_ids < 0) | (col_ids <= row_ids) & (col_ids < length)
    scores = jnp.where(allowed[None], scores, big_negative)
    highest = jnp.max(scores, -1, keepdims=True)
    weights = jnp.exp(scores - highest)
    weights = (weights / jnp.sum(weights, -1, keepdims=True)).astype(jnp.bfloat16)
    mixed = jnp.einsum(
        "hqk,khd->qhd", weights, value_heads, preferred_element_type=jnp.float32
    ).astype(jnp.bfloat16)
    mixed = mixed.reshape(seq_len, -1)
    return jnp.where(row_ids < length, mixed, jnp.zeros_like(mixed))


def slot_ranks(targets, groups):
    onehot = (targets[:, None] == jnp.arange(groups, dtype=jnp.int32)[None, :]).astype(jnp.int32)
    before = jnp.cumsum(onehot, 0) - onehot
    return (jnp.sum(before * onehot, 1), jnp.sum(onehot, 0))


def local(
    patches,
    vis_gain,
    proj_weight,
    image_dest,
    image_pos,
    text_len,
    text,
    attn_gain,
    qkv_weight,
    out_weight,
    cache_keys,
    cache_values,
    held,
    held_owner,
    held_row,
    recompute_pos,
):
    n_req = lax.axis_size("req")
    normed_patch = norm_rows(patches[:, 0, :], vis_gain)
    partial_image = jnp.dot(
        normed_patch,
        lax.all_gather(proj_weight, "req", axis=1, tiled=True)[0],
        preferred_element_type=jnp.float32,
    )
    image_tokens = lax.psum_scatter(partial_image, "mlp", scatter_dimension=1, tiled=True).astype(
        jnp.bfloat16
    )
    img_dev = image_tokens.shape[0]
    capacity = max(2, 2 * img_dev // n_req)
    targets = image_dest[:, 0]
    image_rank, image_counts = slot_ranks(targets, n_req)
    outgoing = (
        jnp.zeros((n_req, capacity, image_tokens.shape[1]), jnp.bfloat16)
        .at[targets, image_rank]
        .set(image_tokens)
    )
    arrived, arrived_counts = (
        lax.all_to_all(outgoing, "req", split_axis=0, concat_axis=0, tiled=True),
        lax.all_to_all(
            image_counts.reshape(n_req, 1), "req", split_axis=0, concat_axis=0, tiled=True
        ),
    )
    filled = (
        (jnp.arange(capacity, dtype=jnp.int32)[None, :] < arrived_counts)
        .reshape(-1)
        .astype(jnp.int32)
    )
    image_order = jnp.cumsum(filled) - filled
    img_count = jnp.sum(filled)
    arrived_rows = arrived.reshape(n_req * capacity, arrived.shape[2])
    arrived_rows = lax.all_gather(arrived_rows, "mlp", axis=1, tiled=True)
    seq_len = text.shape[1]
    spots = jnp.arange(seq_len, dtype=jnp.int32)
    offset = jnp.minimum(image_pos[0], seq_len - img_count)
    in_image = (spots >= offset) & (spots < offset + img_count)
    chooser = ((image_order[None, :] == (spots - offset)[:, None]) & (filled[None, :] > 0)).astype(
        jnp.bfloat16
    )
    image_part = jnp.dot(chooser, arrived_rows, preferred_element_type=jnp.float32).astype(
        jnp.bfloat16
    )
    text_index = jnp.clip(jnp.where(spots < offset, spots, spots - img_count), 0, seq_len - 1)
    prompt = jnp.where(in_image[:, None], image_part, text[0][text_index])
    length = jnp.minimum(seq_len, text_len[0] + img_count)
    normed = norm_rows(prompt, attn_gain)
    weight_cols = lax.all_gather(qkv_weight, "req", axis=1, tiled=True)
    queries = jnp.dot(normed, weight_cols[0], preferred_element_type=jnp.float32).astype(
        jnp.bfloat16
    )
    new_keys = jnp.dot(normed, weight_cols[1], preferred_element_type=jnp.float32).astype(
        jnp.bfloat16
    )
    new_values = jnp.dot(normed, weight_cols[2], preferred_element_type=jnp.float32).astype(
        jnp.bfloat16
    )
    owners = held_owner[0, :, 0]
    fetch_rank, fetch_counts = slot_ranks(owners, n_req)
    recomp = owners.shape[0]
    fetch_cap = max(2, 2 * recomp // n_req)
    wanted_rows = jnp.zeros((n_req, fetch_cap), jnp.int32).at[owners, fetch_rank].set(held_row[0])
    picked = held[lax.all_to_all(wanted_rows, "req", split_axis=0, concat_axis=0, tiled=True)]
    fetched = lax.all_to_all(picked, "req", split_axis=0, concat_axis=0, tiled=True)
    gotten = fetched[owners, fetch_rank]
    held_norm = norm_rows(gotten, attn_gain)
    fresh_keys = jnp.dot(held_norm, weight_cols[1], preferred_element_type=jnp.float32).astype(
        jnp.bfloat16
    )
    fresh_values = jnp.dot(held_norm, weight_cols[2], preferred_element_type=jnp.float32).astype(
        jnp.bfloat16
    )
    keys_now = cache_keys[0].at[recompute_pos[0]].set(fresh_keys)
    values_now = cache_values[0].at[recompute_pos[0]].set(fresh_values)
    mixed = attend(
        queries,
        jnp.concatenate([keys_now, new_keys], 0),
        jnp.concatenate([values_now, new_values], 0),
        length,
    )
    terms = jnp.dot(
        mixed,
        lax.all_gather(out_weight, "req", axis=1, tiled=True),
        preferred_element_type=jnp.float32,
    )
    result = lax.psum_scatter(terms, "mlp", scatter_dimension=1, tiled=True).astype(jnp.bfloat16)
    return result[None]


def solution(mesh):
    in_specs = (
        P("req", "mlp", None),
        P(),
        P("mlp", "req", None),
        P("req", None),
        P("req"),
        P("req"),
        P("req", None, None),
        P(),
        P(None, "req", "mlp"),
        P("mlp", "req"),
        P("req", None, "mlp"),
        P("req", None, "mlp"),
        P("req", None),
        P("req", None, None),
        P("req", None),
        P("req", None),
    )
    out_specs = P("req", None, "mlp")
    return jax.shard_map(local, mesh=mesh, in_specs=in_specs, out_specs=out_specs, check_vma=False)
```

profile of v0, /device:TPU:8, one launch (start us, length us, event | category | flops | bytes accessed | tf_op | source)
XLA Modules:
  0.0 346.3 jit_solution(4919640971527965085)
XLA Ops:
  6.6 1.5 copy.49
  8.2 0.7 all-gather.4.cloned.1.call-update
  8.9 0.7 fusion.39
  9.8 0.8 select_reduce_fusion
  10.7 0.7 copy.44
  11.4 17.4 %all-to-all-start = ((s32[128,1,1]{2,1,0:T(1,128)}), s32[128,1,1]{2,1,0:T(1,128)S(1)}, u32[]{:S(2)}, u32[]{:S(2)}) async-start(s32[128,1,1]{2,1,0:T(1,128)} %copy.44), calls=%async_computation | async-start | bytes 131072 | tf_op jit(solution)/shard_map/all_to_all | solution.py:87
  28.8 0.7 fusion.38
  29.7 0.8 select_reduce_fusion.1
  30.5 1.1 fusion.24
  31.7 52.4 %all-gather = bf16[128,10,320]{2,1,0:T(8,128)(2,1)S(1)} all-gather(bf16[1,10,320]{2,1,0:T(8,128)(2,1)} %bitcast.98), channel_id=1, replica_groups=mesh['req'=128,'mlp'=4] {'req'}, dimensions={0}, use_global_device_ids=true | all-gather | bytes 825600 | tf_op jit(solution)/shard_map/all_gather | solution.py:149
  84.1 0.5 fusion.48
  85.5 6.4 %scatter_fusion = s32[128,2]{0,1:T(2,128)S(1)} fusion(s32[128,2]{0,1:T(2,128)S(1)} %broadcast.276, s32[128]{0:T(128)S(1)} %get-tuple-element.7, s32[128]{0:T(128)S(1)} %bitcast.105), kind=kCustom, calls=%fused_computation.3 | custom fusion | bytes 2560 | tf_op jit(solution)/shard_map/scatter | solution.py:128
  91.8 0.7 copy.46
  92.6 1.3 copy.55
  94.5 2.3 copy.45
  96.8 1.4 reshape.394
  98.2 10.5 %all-to-all-start.1 = ((s32[128,1,2]{2,1,0:T(1,128)}), s32[128,1,2]{2,1,0:T(1,128)S(1)}, u32[]{:S(2)}, u32[]{:S(2)}) async-start(s32[128,1,2]{2,1,0:T(1,128)} %copy.46), calls=%async_computation.1 | async-start | bytes 131072 | tf_op jit(solution)/shard_map/all_to_all | solution.py:129
  108.7 2.4 reduce.2
  111.4 0.7 fusion.42
  112.9 0.7 compare_select_fusion.1
  113.6 5.9 %all-to-all-done.1 = s32[128,1,2]{2,1,0:T(1,128)S(1)} async-done(((s32[128,1,2]{2,1,0:T(1,128)}), s32[128,1,2]{2,1,0:T(1,128)S(1)}, u32[]{:S(2)}, u32[]{:S(2)}) %all-to-all-start.1) | async-done | bytes 1056 | tf_op jit(solution)/shard_map/all_to_all | solution.py:129
  119.7 1.3 gather_fusion
  120.9 1.1 reshape.343
  122.0 7.8 %all-to-all-start.2 = ((bf16[128,2,1280]{2,1,0:T(2,128)(2,1)}), bf16[128,2,1280]{2,1,0:T(2,128)(2,1)S(1)}, u32[]{:S(2)}, u32[]{:S(2)}) async-start(bf16[128,2,1280]{2,1,0:T(2,128)(2,1)} %reshape.343), calls=%async_computation.2 | async-start | bytes 1310720 | tf_op jit(solution)/shard_map/all_to_all | solution.py:130
  131.8 2.1 gather_fusion.2
  133.9 0.5 iota_compare_fusion.4
  134.5 0.5 compare_and_fusion
  135.1 0.5 bitcast_subtract_fusion
  135.6 1.1 fusion.12
  136.7 16.5 %all-to-all-done.2 = bf16[128,2,1280]{2,1,0:T(2,128)(2,1)S(1)} async-done(((bf16[128,2,1280]{2,1,0:T(2,128)(2,1)}), bf16[128,2,1280]{2,1,0:T(2,128)(2,1)S(1)}, u32[]{:S(2)}, u32[]{:S(2)}) %all-to-all-start.2) | async-done | bytes 655392 | tf_op jit(solution)/shard_map/all_to_all | solution.py:130
  153.2 1.5 gather_fusion.1
  154.8 0.5 add_rsqrt_fusion.2
  155.4 5.1 %fusion.2 = f32[128,1280]{0,1:T(8,128)} fusion(bf16[1,1280,1280]{2,0,1:T(2,128)(2,1)} %all-gather.6.cloned.1.call-done, bf16[128,1,1280]{2,0,1:T(8,128)(2,1)S(1)} %copy-done.15, f32[1280]{0:T(1024)S(1)} %copy-done.26, f32[128]{0:T(128)S(1)} %add_rsqrt_fusion.1), kind=kOutput, calls=%fused_computation.12 | convolution fusion | flops 420085760 | bytes 4265472 | tf_op jit(solution)/shard_map/dot_general | solution.py:68
  160.5 33.4 %all-gather.4.cloned.1.call-done = bf16[3,1280,320]{2,0,1:T(4,128)(2,1)} async-done(((bf16[3,10,320]{2,0,1:T(4,128)(2,1)}), bf16[3,1280,320]{2,0,1:T(4,128)(2,1)}) %all-gather.4.cloned.1.call-update) | async-done | bytes 2457616 | tf_op jit(solution)/shard_map/all_gather | solution.py:114
  194.0 10.7 %fusion.59 = (bf16[1,1280,320]{2,0,1:T(2,128)(2,1)}, bf16[1,1280,320]{2,0,1:T(2,128)(2,1)}, bf16[1,1280,320]{2,0,1:T(2,128)(2,1)S(1)}) fusion(bf16[3,1280,320]{2,0,1:T(4,128)(2,1)} %all-gather.4.cloned.1.call-done), kind=kLoop, calls=%fused_computation.111 | loop fusion | bytes 4915200 | tf_op jit(solution)/shard_map/slice | solution.py:133
  204.7 3.9 %copy.63 = bf16[1,1280,320]{1,2,0:T(8,128)(2,1)S(1)} copy(bf16[1,1280,320]{2,0,1:T(2,128)(2,1)} %get-tuple-element.9) | data formatting | bytes 1638400
  208.6 12.9 %reduce-scatter.3.cloned.1.call-done = f32[128,320]{0,1:T(8,128)} async-done(((f32[128,1280]{0,1:T(8,128)}), f32[128,320]{0,1:T(8,128)}) %reduce-scatter.3.cloned.1.call-update) | async-done | bytes 163856 | tf_op jit(solution)/shard_map/reduce_scatter | solution.py:73
  221.5 1.6 convert_element_type.94
  223.0 1.0 copy.50
  224.0 0.8 broadcast_in_dim.29
  224.8 15.1 %scatter_fusion.2 = bf16[128,2,320]{2,1,0:T(2,128)(2,1)} fusion(bf16[128,2,320]{2,1,0:T(2,128)(2,1)} %broadcast_in_dim.29, s32[128]{0:T(128)S(1)} %fusion.50, bf16[128,320]{1,0:T(8,128)(2,1)S(1)} %copy.50), kind=kCustom, calls=%fused_computation.5 | custom fusion | bytes 246784 | tf_op jit(solution)/shard_map/scatter | solution.py:83
  239.9 14.7 %all-to-all-start.3 = ((bf16[128,2,320]{2,1,0:T(2,128)(2,1)}), bf16[128,2,320]{2,1,0:T(2,128)(2,1)}, u32[]{:S(2)}, u32[]{:S(2)}) async-start(bf16[128,2,320]{2,1,0:T(2,128)(2,1)} %scatter_fusion.2), calls=%async_computation.4 | async-start | bytes 393216 | tf_op jit(solution)/shard_map/all_to_all | solution.py:86
  254.7 2.1 convolution_convert_fusion.4
  256.7 1.0 copy.57
  257.7 4.9 %copy.62 = bf16[1,1280,320]{1,2,0:T(8,128)(2,1)} copy(bf16[1,1280,320]{2,0,1:T(2,128)(2,1)} %get-tuple-element.10) | data formatting | bytes 1638400
  262.6 2.8 copy.61
  265.4 1.7 convolution_convert_fusion.5
  267.3 3.5 %scatter_fusion.3 = bf16[1280,320]{1,0:T(8,128)(2,1)} fusion(bf16[1280,320]{1,0:T(8,128)(2,1)} %bitcast.91, s32[128]{0:T(128)} %fusion.48, bf16[128,320]{1,0:T(8,128)(2,1)S(1)} %copy.57), kind=kCustom, calls=%fused_computation.6 | custom fusion | bytes 246272 | tf_op jit(solution)/shard_map/scatter | solution.py:139
  270.8 1.6 scatter_fusion.1
  272.5 1.1 reshape.336
  273.7 13.8 %all_gather.14 = bf16[256,1280]{0,1:T(8,128)(2,1)S(1)} all-gather(bf16[256,320]{0,1:T(8,128)(2,1)S(1)} %copy.51), channel_id=1, replica_groups=mesh['req'=128,'mlp'=4] {'mlp'}, dimensions={1}, use_global_device_ids=true | all-gather | bytes 819200 | tf_op jit(solution)/shard_map/all_gather | solution.py:99
  287.5 0.5 multiply_reduce_fusion
  288.6 1.1 convolution_convert_fusion.1
  289.7 1.1 convolution_convert_fusion.3
  290.8 1.1 copy.58
  291.9 1.1 pad_maximum_fusion.1
  293.0 2.4 copy.59
  295.4 2.2 convolution_convert_fusion.2
  297.9 1.4 copy.53
  299.3 3.7 %fusion.60 = f32[4,256]{1,0:T(4,128)S(1)} fusion(pred[256,1536]{1,0:T(8,128)(4,1)S(1)} %copy-done.14, bf16[256,4,80]{0,2,1:T(8,128)(2,1)} %bitcast.96, bf16[1536,4,80]{0,2,1:T(8,128)(2,1)} %bitcast.92), kind=kOutput, calls=%fused_computation.112 | convolution fusion | flops 257951232 | bytes 1544192 | tf_op jit(solution)/shard_map/sub | solution.py:33
  303.1 3.9 %fusion.13 = bf16[4,80,256]{2,1,0:T(8,128)(2,1)S(1)} fusion(bf16[1536,4,80]{0,2,1:T(8,128)(2,1)} %bitcast.94, f32[4,256]{1,0:T(4,128)S(1)} %fusion.60, pred[256,1536]{1,0:T(8,128)(4,1)S(1)} %copy-done.14, bf16[256,4,80]{0,2,1:T(8,128)(2,1)S(1)} %bitcast.97, bf16[1536,4,80]{0,2,1:T(8,128)(2,1)S(1)} %bitcast.93), kind=kOutput, calls=%fused_computation.29 | convolution fusion | flops 511265280 | bytes 2691072 | tf_op jit(solution)/shard_map/hqk,khd->qhd/dot_general | solution.py:35
  307.1 1.6 fusion.61
  308.7 29.4 %reduce-scatter.5.cloned.1.call-done = f32[256,320]{0,1:T(8,128)} async-done(((f32[256,1280]{0,1:T(8,128)}), f32[256,320]{0,1:T(8,128)}) %reduce-scatter.5.cloned.1.call-update) | async-done | bytes 327696 | tf_op jit(solution)/shard_map/reduce_scatter | solution.py:152
  338.1 1.7 convert_bitcast_fusion
  (98 shorter events, 3.4 us)
Async XLA Ops:
  6.5 125.2 %copy-start = (bf16[1,256,1280]{2,1,0:T(8,128)(2,1)S(1)}, bf16[1,256,1280]{2,1,0:T(8,128)(2,1)}, u32[]{:S(2)}) copy-start(bf16[1,256,1280]{2,1,0:T(8,128)(2,1)} %param.22) | copy-start | bytes 1966084
  6.5 78.1 %copy-start.20 = (s32[128,1]{0,1:T(1,128)S(1)}, s32[128,1]{0,1:T(1,128)}, u32[]{:S(2)}) copy-start(s32[128,1]{0,1:T(1,128)} %param.19) | copy-start | bytes 1540
  6.5 78.1 %copy-start.18 = (s32[1,128,1]{1,2,0:T(1,128)S(1)}, s32[1,128,1]{1,2,0:T(1,128)}, u32[]{:S(2)}) copy-start(s32[1,128,1]{1,2,0:T(1,128)} %param.29) | copy-start | bytes 1540
  6.5 77.6 %copy-start.27 = (s32[1,128]{1,0:T(1,128)S(1)}, s32[1,128]{1,0:T(1,128)}, u32[]{:S(2)}) copy-start(s32[1,128]{1,0:T(1,128)} %param.31) | copy-start | bytes 1540
  6.5 78.9 %copy-start.24 = (s32[1,128]{1,0:T(1,128)S(1)}, s32[1,128]{1,0:T(1,128)}, u32[]{:S(2)}) copy-start(s32[1,128]{1,0:T(1,128)} %param.30) | copy-start | bytes 1540
  6.5 86.0 %copy-start.12 = (bf16[1,1280,320]{1,2,0:T(8,128)(2,1)S(1)}, bf16[1,1280,320]{1,2,0:T(8,128)(2,1)}, u32[]{:S(2)}) copy-start(bf16[1,1280,320]{1,2,0:T(8,128)(2,1)} %param.26) | copy-start | bytes 2457604
  6.6 148.8 %all-gather.6.cloned.1.call-start = ((), (), s32[]{:S(2)}) async-start(), calls=%async_computation.7 | async-start | bytes 6604800 | tf_op jit(solution)/shard_map/all_gather | solution.py:70
  8.2 185.8 %all-gather.4.cloned.1.call-start = ((), (), s32[]{:S(2)}) async-start(), calls=%async_computation.6 | async-start | bytes 3962880 | tf_op jit(solution)/shard_map/all_gather | solution.py:114
  11.4 86.8 %all-to-all-start = ((s32[128,1,1]{2,1,0:T(1,128)}), s32[128,1,1]{2,1,0:T(1,128)S(1)}, u32[]{:S(2)}, u32[]{:S(2)}) async-start(s32[128,1,1]{2,1,0:T(1,128)} %copy.44), calls=%async_computation | async-start | bytes 131072 | tf_op jit(solution)/shard_map/all_to_all | solution.py:87
  94.5 25.1 %copy-start.1 = (bf16[128,1280]{1,0:T(8,128)(2,1)S(1)}, bf16[128,1280]{1,0:T(8,128)(2,1)}, u32[]{:S(2)}) copy-start(bf16[128,1280]{1,0:T(8,128)(2,1)} %param.28) | copy-start | bytes 983044
  98.2 21.2 %all-to-all-start.1 = ((s32[128,1,2]{2,1,0:T(1,128)}), s32[128,1,2]{2,1,0:T(1,128)S(1)}, u32[]{:S(2)}, u32[]{:S(2)}) async-start(s32[128,1,2]{2,1,0:T(1,128)} %copy.46), calls=%async_computation.1 | async-start | bytes 131072 | tf_op jit(solution)/shard_map/all_to_all | solution.py:129
  122.0 31.2 %all-to-all-start.2 = ((bf16[128,2,1280]{2,1,0:T(2,128)(2,1)}), bf16[128,2,1280]{2,1,0:T(2,128)(2,1)S(1)}, u32[]{:S(2)}, u32[]{:S(2)}) async-start(bf16[128,2,1280]{2,1,0:T(2,128)(2,1)} %reshape.343), calls=%async_computation.2 | async-start | bytes 1310720 | tf_op jit(solution)/shard_map/all_to_all | solution.py:130
  129.8 91.6 %reduce-scatter.3.cloned.1.call-start = ((), (), s32[]{:S(2)}) async-start(), calls=%async_computation.8 | async-start | bytes 819200 | tf_op jit(solution)/shard_map/reduce_scatter | solution.py:73
  133.9 21.5 %copy-start.15 = (bf16[128,1,1280]{2,0,1:T(8,128)(2,1)S(1)}, bf16[128,1,1280]{2,0,1:T(8,128)(2,1)}, u32[]{:S(2)}) copy-start(bf16[128,1,1280]{2,0,1:T(8,128)(2,1)} %param.16) | copy-start | bytes 983044
  133.9 21.5 %copy-start.26 = (f32[1280]{0:T(1024)S(1)}, f32[1280]{0:T(1024)}, u32[]{:S(2)}) copy-start(f32[1280]{0:T(1024)} %param.17) | copy-start | bytes 15364
  154.7 5.8 %copy-start.10 = (bf16[128,1280]{1,0:T(8,128)(2,1)}, bf16[128,1280]{1,0:T(8,128)(2,1)S(1)}, u32[]{:S(2)}) copy-start(bf16[128,1280]{1,0:T(8,128)(2,1)S(1)} %gather_fusion.1) | copy-start | bytes 983044
  204.7 50.0 %copy-start.17 = (f32[1280]{0:T(1024)S(1)}, f32[1280]{0:T(1024)}, u32[]{:S(2)}) copy-start(f32[1280]{0:T(1024)} %param.23) | copy-start | bytes 15364
  208.6 54.0 %copy-start.5 = (bf16[1,1280,320]{1,2,0:T(8,128)(2,1)}, bf16[1,1280,320]{1,2,0:T(8,128)(2,1)S(1)}, u32[]{:S(2)}) copy-start(bf16[1,1280,320]{1,2,0:T(8,128)(2,1)S(1)} %copy.63) | copy-start | bytes 2457604
  239.9 32.6 %all-to-all-start.3 = ((bf16[128,2,320]{2,1,0:T(2,128)(2,1)}), bf16[128,2,320]{2,1,0:T(2,128)(2,1)}, u32[]{:S(2)}, u32[]{:S(2)}) async-start(bf16[128,2,320]{2,1,0:T(2,128)(2,1)} %scatter_fusion.2), calls=%async_computation.4 | async-start | bytes 393216 | tf_op jit(solution)/shard_map/all_to_all | solution.py:86
  254.6 83.5 %reduce-scatter.5.cloned.1.call-start = ((), (), s32[]{:S(2)}) async-start(), calls=%async_computation.9 | async-start | bytes 1638400 | tf_op jit(solution)/shard_map/reduce_scatter | solution.py:152
  265.4 7.1 %copy-start.7 = (bf16[1,1280,320]{1,2,0:T(8,128)(2,1)}, bf16[1,1280,320]{1,2,0:T(8,128)(2,1)S(1)}, u32[]{:S(2)}) copy-start(bf16[1,1280,320]{1,2,0:T(8,128)(2,1)S(1)} %copy.61) | copy-start | bytes 2457604
  265.4 5.4 %copy-start.2 = (bf16[1,1280,320]{2,1,0:T(8,128)(2,1)S(1)}, bf16[1,1280,320]{2,1,0:T(8,128)(2,1)}, u32[]{:S(2)}) copy-start(bf16[1,1280,320]{2,1,0:T(8,128)(2,1)} %copy.45) | copy-start | bytes 2457604
  265.4 5.4 %copy-start.21 = (s32[128]{0:T(128)S(1)}, s32[128]{0:T(128)}, u32[]{:S(2)}) copy-start(s32[128]{0:T(128)} %fusion.48) | copy-start | bytes 1540
  267.3 20.2 %copy-start.9 = (bf16[256,1280]{1,0:T(8,128)(2,1)S(1)}, bf16[256,1280]{1,0:T(8,128)(2,1)}, u32[]{:S(2)}) copy-start(bf16[256,1280]{1,0:T(8,128)(2,1)} %gather_fusion.2) | copy-start | bytes 1966084
  270.8 16.7 %copy-start.19 = (s32[256]{0:T(256)S(1)}, s32[256]{0:T(256)}, u32[]{:S(2)}) copy-start(s32[256]{0:T(256)} %get-tuple-element.17) | copy-start | bytes 3076
  270.8 16.7 %copy-start.22 = (pred[256]{0:T(512)(128)(4,1)S(1)}, pred[256]{0:T(512)(128)(4,1)}, u32[]{:S(2)}) copy-start(pred[256]{0:T(512)(128)(4,1)} %get-tuple-element.14) | copy-start | bytes 772
  270.8 16.7 %copy-start.23 = (pred[256]{0:T(512)(128)(4,1)S(1)}, pred[256]{0:T(512)(128)(4,1)}, u32[]{:S(2)}) copy-start(pred[256]{0:T(512)(128)(4,1)} %get-tuple-element.15) | copy-start | bytes 772
  287.5 1.1 copy-start.6
  288.0 1.7 copy-start.8
  288.0 3.9 %copy-start.3 = (bf16[1280,320]{1,0:T(8,128)(2,1)S(1)}, bf16[1280,320]{1,0:T(8,128)(2,1)}, u32[]{:S(2)}) copy-start(bf16[1280,320]{1,0:T(8,128)(2,1)} %scatter_fusion.3) | copy-start | bytes 2457604
  293.0 4.6 %copy-start.13 = (bf16[256,320]{0,1:T(8,128)(2,1)S(1)}, bf16[256,320]{0,1:T(8,128)(2,1)}, u32[]{:S(2)}) copy-start(bf16[256,320]{0,1:T(8,128)(2,1)} %convolution_convert_fusion.3) | copy-start | bytes 491524
  297.6 1.7 copy-start.14
  299.3 3.7 %copy-start.11 = (bf16[1536,320]{0,1:T(8,128)(2,1)S(1)}, bf16[1536,320]{0,1:T(8,128)(2,1)}, u32[]{:S(2)}) copy-start(bf16[1536,320]{0,1:T(8,128)(2,1)} %copy.59) | copy-start | bytes 2949124
  299.3 3.8 %copy-start.16 = (bf16[256,320]{0,1:T(8,128)(2,1)S(1)}, bf16[256,320]{0,1:T(8,128)(2,1)}, u32[]{:S(2)}) copy-start(bf16[256,320]{0,1:T(8,128)(2,1)} %convolution_convert_fusion.2) | copy-start | bytes 491524
  303.1 4.0 %copy-start.25 = (pred[256]{0:T(512)(128)(4,1)S(1)}, pred[256]{0:T(512)(128)(4,1)}, u32[]{:S(2)}) copy-start(pred[256]{0:T(512)(128)(4,1)} %iota_compare_fusion.4) | copy-start | bytes 772
  303.1 4.0 %copy-start.4 = (bf16[1280,320]{1,0:T(8,128)(2,1)S(1)}, bf16[1280,320]{1,0:T(8,128)(2,1)}, u32[]{:S(2)}) copy-start(bf16[1280,320]{1,0:T(8,128)(2,1)} %reshape.394) | copy-start | bytes 2457604
Sparse Core Ops, SparseCore 0:
  10.6 91.5 all-gather.5
  105.4 88.5 all-gather.3
  196.8 24.6 reduce-scatter.2
  308.8 29.2 reduce-scatter.4
where the time goes:
time: 348 us; the launch traced here: 346 us
  waiting for transfers between devices  98.9 us (28%)
  local copies, waits for them, and re-layouts  73.4 us (21%)
  blocking collectives  66.2 us (19%)
  starting transfers between devices  50.5 us (15%)
  matrix products  23 us (7%)
  other arithmetic  17.4 us (5%)
  between operations  16.9 us (5%)
    all_gather x1, blocking collectives, local(): lax.all_gather(out_weight, 'req', axis=1, tiled=True)  52.4 us
    all_gather x1, waiting for transfers between devices, local(): weight_cols = lax.all_gather(qkv_weight, 'req', axis=1, tiled=True)  33.4 us
    reduce_scatter x1, waiting for transfers between devices, local(): lax.psum_scatter(terms, 'mlp', scatter_dimension=1, tiled=True)  29.4 us
    unnamed x63, local copies, waits for them, and re-layouts  18.6 us
    all_to_all x1, starting transfers between devices, local(): lax.all_to_all(image_counts.reshape(n_req, 1), 'req', split_axis=0, conca...  17.4 us
    all_to_all x1, waiting for transfers between devices, local(): lax.all_to_all(picked, 'req', split_axis=0, concat_axis=0, tiled=True)  16.5 us
    scatter x1, local copies, waits for them, and re-layouts, local(): outgoing = jnp.zeros((n_req, capacity, image_tokens.shape[1]), jnp.bfloat...  15.1 us
    all_to_all x1, starting transfers between devices, local(): lax.all_to_all(outgoing, 'req', split_axis=0, concat_axis=0, tiled=True)  14.7 us
  transfers between devices with their start and end apart: 8, of which 5 were waited for; matrix products, arithmetic and copies ran while one was open for 20% of the time, Pallas kernels for 0%

commit v1 on v0

--- a/solution.py
+++ b/solution.py
@@ -146,7 +146,9 @@
     )
     terms = jnp.dot(
         mixed,
-        lax.all_gather(out_weight, "req", axis=1, tiled=True),
+        jnp.concatenate(
+            lax.all_to_all(jnp.stack([out_weight] * lax.axis_size("req")), "req", 0, 0), axis=1
+        ),
         preferred_element_type=jnp.float32,
     )
     result = lax.psum_scatter(terms, "mlp", scatter_dimension=1, tiled=True).astype(jnp.bfloat16)

time: 348 us -> 366 us (1.052)
  waiting for transfers between devices: 98.9 us -> 157 us
  blocking collectives: 66.2 us -> 13.8 us
  starting transfers between devices: 50.5 us -> 57.1 us
  local copies, waits for them, and re-layouts: 73.4 us -> 78.4 us
    all_gather x1 -> x0, blocking collectives: 52.4 us -> none  [local(): lax.all_gather(out_weight, 'req', axis=1, tiled=True)]
    all_to_all x0 -> x1, waiting for transfers between devices: none -> 33.7 us  [local(): lax.all_to_all(jnp.stack([out_weight] * lax.axis_size('req')), 'req', 0, 0)]
    all_gather x1, waiting for transfers between devices: 33.4 us -> 46.9 us  [local(): weight_cols = lax.all_gather(qkv_weight, 'req', axis=1, tiled=True)]
    all_to_all x1, waiting for transfers between devices: 0.01 us -> 8.16 us  [local(): lax.all_to_all(image_counts.reshape(n_req, 1), 'req', split_axis=0, conca...]
    all_to_all x0 -> x1, starting transfers between devices: none -> 7.74 us  [local(): lax.all_to_all(jnp.stack([out_weight] * lax.axis_size('req')), 'req', 0, 0)]
    all_to_all x1, starting transfers between devices: 10.5 us -> 17.4 us  [local(): lax.all_to_all(wanted_rows, 'req', split_axis=0, concat_axis=0, tiled=True)]
    all_to_all x1, starting transfers between devices: 17.4 us -> 10.8 us  [local(): lax.all_to_all(image_counts.reshape(n_req, 1), 'req', split_axis=0, conca...]
    all_to_all x1, waiting for transfers between devices: 16.5 us -> 21.9 us  [local(): lax.all_to_all(picked, 'req', split_axis=0, concat_axis=0, tiled=True)]
  transfers between devices with their start and end apart: 8 -> 9, of which waited for: 5 -> 7; matrix products, arithmetic and copies ran while one was open for 20% -> 21% of each run, Pallas kernels for 0% -> 0%
where the time goes in v1:
time: 366 us; the launch traced here: 365 us
  waiting for transfers between devices  157 us (43%)
  local copies, waits for them, and re-layouts  78.4 us (21%)
  starting transfers between devices  57.1 us (16%)
  matrix products  23 us (6%)
  other arithmetic  18.9 us (5%)
  between operations  16.9 us (5%)
  blocking collectives  13.8 us (4%)
    all_gather x1, waiting for transfers between devices, local(): weight_cols = lax.all_gather(qkv_weight, 'req', axis=1, tiled=True)  46.9 us
    all_to_all x1, waiting for transfers between devices, local(): lax.all_to_all(jnp.stack([out_weight] * lax.axis_size('req')), 'req', 0, 0)  33.7 us
    reduce_scatter x1, waiting for transfers between devices, local(): lax.psum_scatter(terms, 'mlp', scatter_dimension=1, tiled=True)  29.4 us
    all_to_all x1, waiting for transfers between devices, local(): lax.all_to_all(picked, 'req', split_axis=0, concat_axis=0, tiled=True)  21.9 us
    all_to_all x1, starting transfers between devices, local(): lax.all_to_all(wanted_rows, 'req', split_axis=0, concat_axis=0, tiled=True)  17.4 us
    unnamed x68, local copies, waits for them, and re-layouts  16.3 us
    scatter x1, local copies, waits for them, and re-layouts, local(): outgoing = jnp.zeros((n_req, capacity, image_tokens.shape[1]), jnp.bfloat...  15.1 us
    all_to_all x1, starting transfers between devices, local(): lax.all_to_all(outgoing, 'req', split_axis=0, concat_axis=0, tiled=True)  14.4 us
  transfers between devices with their start and end apart: 9, of which 7 were waited for; matrix products, arithmetic and copies ran while one was open for 21% of the time, Pallas kernels for 0%

profile of v1, /device:TPU:8, one launch (start us, length us, event | category | flops | bytes accessed | tf_op | source)
XLA Modules:
  0.0 364.7 jit_solution(17063799169374356126)
XLA Ops:
  6.5 1.6 copy.50
  8.2 0.7 all-gather.3.cloned.1.call-update
  8.9 0.7 fusion.39
  9.8 0.8 select_reduce_fusion.1
  10.7 0.7 fusion.52
  11.3 11.0 %scatter_fusion = s32[128,2]{0,1:T(2,128)S(1)} fusion(s32[128,2]{0,1:T(2,128)S(1)} %broadcast.286, s32[128]{0:T(128)S(1)} %get-tuple-element.7, s32[128]{0:T(128)} %bitcast.105), kind=kCustom, calls=%fused_computation.3 | custom fusion | bytes 2560 | tf_op jit(solution)/shard_map/scatter | solution.py:128
  22.3 0.7 copy.47
  23.0 17.4 %all-to-all-start.1 = ((s32[128,1,2]{2,1,0:T(1,128)}), s32[128,1,2]{2,1,0:T(1,128)S(1)}, u32[]{:S(2)}, u32[]{:S(2)}) async-start(s32[128,1,2]{2,1,0:T(1,128)} %copy.47), calls=%async_computation.1 | async-start | bytes 131072 | tf_op jit(solution)/shard_map/all_to_all | solution.py:129
  40.4 0.8 fusion.40
  41.4 0.8 select_reduce_fusion
  42.2 1.1 fusion.25
  43.4 0.7 copy.45
  44.9 1.3 copy.56
  46.9 1.3 copy.46
  48.2 2.9 all-to-all-done.1
  51.1 10.8 %all-to-all-start = ((s32[128,1,1]{2,1,0:T(1,128)}), s32[128,1,1]{2,1,0:T(1,128)S(1)}, u32[]{:S(2)}, u32[]{:S(2)}) async-start(s32[128,1,1]{2,1,0:T(1,128)} %copy.45), calls=%async_computation | async-start | bytes 131072 | tf_op jit(solution)/shard_map/all_to_all | solution.py:87
  62.1 1.3 gather_fusion
  63.4 1.1 reshape.356
  64.5 8.2 %all-to-all-done = s32[128,1,1]{2,1,0:T(1,128)S(1)} async-done(((s32[128,1,1]{2,1,0:T(1,128)}), s32[128,1,1]{2,1,0:T(1,128)S(1)}, u32[]{:S(2)}, u32[]{:S(2)}) %all-to-all-start) | async-done | bytes 544 | tf_op jit(solution)/shard_map/all_to_all | solution.py:87
  72.7 6.4 %all-to-all-start.2 = ((bf16[128,2,1280]{2,1,0:T(2,128)(2,1)}), bf16[128,2,1280]{2,1,0:T(2,128)(2,1)S(1)}, u32[]{:S(2)}, u32[]{:S(2)}) async-start(bf16[128,2,1280]{2,1,0:T(2,128)(2,1)} %reshape.356), calls=%async_computation.2 | async-start | bytes 1310720 | tf_op jit(solution)/shard_map/all_to_all | solution.py:130
  80.3 2.4 reduce.2
  83.0 0.7 fusion.43
  84.3 0.7 compare_select_fusion.1
  85.1 21.9 %all-to-all-done.2 = bf16[128,2,1280]{2,1,0:T(2,128)(2,1)S(1)} async-done(((bf16[128,2,1280]{2,1,0:T(2,128)(2,1)}), bf16[128,2,1280]{2,1,0:T(2,128)(2,1)S(1)}, u32[]{:S(2)}, u32[]{:S(2)}) %all-to-all-start.2) | async-done | bytes 655392 | tf_op jit(solution)/shard_map/all_to_all | solution.py:130
  107.0 1.3 stack.2
  108.3 7.7 %all-to-all-start.4 = ((bf16[128,320,10]{1,2,0:T(8,128)(2,1)}), bf16[128,320,10]{1,2,0:T(8,128)(2,1)S(1)}, u32[]{:S(2)}, u32[]{:S(2)}) async-start(bf16[128,320,10]{1,2,0:T(8,128)(2,1)} %stack.2), calls=%async_computation.5 | async-start | bytes 3145728 | tf_op jit(solution)/shard_map/all_to_all | solution.py:150
  117.9 2.1 gather_fusion.2
  121.3 0.7 bitcast_subtract_fusion
  121.9 1.1 fusion.12
  123.0 1.5 gather_fusion.1
  124.7 0.6 add_rsqrt_fusion.2
  125.3 33.7 %all-to-all-done.4 = bf16[128,320,10]{1,2,0:T(8,128)(2,1)S(1)} async-done(((bf16[128,320,10]{1,2,0:T(8,128)(2,1)}), bf16[128,320,10]{1,2,0:T(8,128)(2,1)S(1)}, u32[]{:S(2)}, u32[]{:S(2)}) %all-to-all-start.4) | async-done | bytes 819232 | tf_op jit(solution)/shard_map/all_to_all | solution.py:150
  159.0 1.4 reshape.353
  160.4 5.1 %fusion.2 = f32[128,1280]{0,1:T(8,128)} fusion(bf16[1,1280,1280]{2,0,1:T(2,128)(2,1)} %all-gather.5.cloned.1.call-done, bf16[128,1,1280]{2,0,1:T(8,128)(2,1)S(1)} %copy-done.16, f32[1280]{0:T(1024)S(1)} %copy-done.26, f32[128]{0:T(128)S(1)} %copy-done.29), kind=kOutput, calls=%fused_computation.12 | convolution fusion | flops 420085760 | bytes 4265472 | tf_op jit(solution)/shard_map/dot_general | solution.py:68
  165.6 46.9 %all-gather.3.cloned.1.call-done = bf16[3,1280,320]{2,0,1:T(4,128)(2,1)} async-done(((bf16[3,10,320]{2,0,1:T(4,128)(2,1)}), bf16[3,1280,320]{2,0,1:T(4,128)(2,1)}) %all-gather.3.cloned.1.call-update) | async-done | bytes 2457616 | tf_op jit(solution)/shard_map/all_gather | solution.py:114
  212.5 10.7 %fusion.60 = (bf16[1,1280,320]{2,0,1:T(2,128)(2,1)}, bf16[1,1280,320]{2,0,1:T(2,128)(2,1)}, bf16[1,1280,320]{2,0,1:T(2,128)(2,1)S(1)}) fusion(bf16[3,1280,320]{2,0,1:T(4,128)(2,1)} %all-gather.3.cloned.1.call-done), kind=kLoop, calls=%fused_computation.111 | loop fusion | bytes 4915200 | tf_op jit(solution)/shard_map/slice | solution.py:133
  223.2 3.9 %copy.64 = bf16[1,1280,320]{1,2,0:T(8,128)(2,1)S(1)} copy(bf16[1,1280,320]{2,0,1:T(2,128)(2,1)} %get-tuple-element.9) | data formatting | bytes 1638400
  227.1 12.9 %reduce-scatter.3.cloned.1.call-done = f32[128,320]{0,1:T(8,128)} async-done(((f32[128,1280]{0,1:T(8,128)}), f32[128,320]{0,1:T(8,128)}) %reduce-scatter.3.cloned.1.call-update) | async-done | bytes 163856 | tf_op jit(solution)/shard_map/reduce_scatter | solution.py:73
  240.0 1.6 convert_element_type.92
  241.5 1.0 copy.51
  242.5 0.8 broadcast_in_dim.29
  243.3 15.1 %scatter_fusion.2 = bf16[128,2,320]{2,1,0:T(2,128)(2,1)} fusion(bf16[128,2,320]{2,1,0:T(2,128)(2,1)} %broadcast_in_dim.29, s32[128]{0:T(128)S(1)} %fusion.51, bf16[128,320]{1,0:T(8,128)(2,1)S(1)} %copy.51), kind=kCustom, calls=%fused_computation.5 | custom fusion | bytes 246784 | tf_op jit(solution)/shard_map/scatter | solution.py:83
  258.4 14.4 %all-to-all-start.3 = ((bf16[128,2,320]{2,1,0:T(2,128)(2,1)}), bf16[128,2,320]{2,1,0:T(2,128)(2,1)}, u32[]{:S(2)}, u32[]{:S(2)}) async-start(bf16[128,2,320]{2,1,0:T(2,128)(2,1)} %scatter_fusion.2), calls=%async_computation.4 | async-start | bytes 393216 | tf_op jit(solution)/shard_map/all_to_all | solution.py:86
  273.1 2.1 convolution_convert_fusion.4
  275.2 1.0 copy.58
  276.2 4.9 %copy.63 = bf16[1,1280,320]{1,2,0:T(8,128)(2,1)} copy(bf16[1,1280,320]{2,0,1:T(2,128)(2,1)} %get-tuple-element.10) | data formatting | bytes 1638400
  281.0 2.8 copy.62
  283.8 1.7 convolution_convert_fusion.5
  285.7 3.5 scatter_fusion.3
  289.3 1.6 scatter_fusion.1
  291.0 1.1 reshape.348
  292.2 13.8 %all_gather.11 = bf16[256,1280]{0,1:T(8,128)(2,1)S(1)} all-gather(bf16[256,320]{0,1:T(8,128)(2,1)S(1)} %copy.52), channel_id=1, replica_groups=mesh['req'=128,'mlp'=4] {'mlp'}, dimensions={1}, use_global_device_ids=true | all-gather | bytes 819200 | tf_op jit(solution)/shard_map/all_gather | solution.py:99
  307.1 1.1 convolution_convert_fusion.1
  308.2 1.1 convolution_convert_fusion.3
  309.2 1.1 copy.59
  310.3 1.1 pad_maximum_fusion.1
  311.5 2.4 copy.60
  313.8 2.2 convolution_convert_fusion.2
  316.4 1.4 copy.54
  317.8 3.7 %fusion.61 = f32[4,256]{1,0:T(4,128)S(1)} fusion(pred[256,1536]{1,0:T(8,128)(4,1)S(1)} %copy-done.15, bf16[256,4,80]{0,2,1:T(8,128)(2,1)} %bitcast.97, bf16[1536,4,80]{0,2,1:T(8,128)(2,1)} %bitcast.92), kind=kOutput, calls=%fused_computation.112 | convolution fusion | flops 257951232 | bytes 1544192 | tf_op jit(solution)/shard_map/sub | solution.py:33
  321.6 3.9 %fusion.14 = bf16[4,80,256]{2,1,0:T(8,128)(2,1)S(1)} fusion(bf16[1536,4,80]{0,2,1:T(8,128)(2,1)} %bitcast.94, f32[4,256]{1,0:T(4,128)S(1)} %fusion.61, pred[256]{0:T(512)(128)(4,1)S(1)} %copy-done.28, pred[256,1536]{1,0:T(8,128)(4,1)S(1)} %copy-done.15, bf16[256,4,80]{0,2,1:T(8,128)(2,1)S(1)} %bitcast.98, bf16[1536,4,80]{0,2,1:T(8,128)(2,1)S(1)} %bitcast.93), kind=kOutput, calls=%fused_computation.35 | convolution fusion | flops 511347200 | bytes 2691328 | tf_op jit(solution)/shard_map/hqk,khd->qhd/dot_general | solution.py:35
  325.6 1.6 fusion.62
  327.1 29.4 %reduce-scatter.5.cloned.1.call-done = f32[256,320]{0,1:T(8,128)} async-done(((f32[256,1280]{0,1:T(8,128)}), f32[256,320]{0,1:T(8,128)}) %reduce-scatter.5.cloned.1.call-update) | async-done | bytes 327696 | tf_op jit(solution)/shard_map/reduce_scatter | solution.py:154
  356.5 1.7 convert_bitcast_fusion
  (105 shorter events, 6.3 us)
Async XLA Ops:
  6.5 111.4 %copy-start = (bf16[1,256,1280]{2,1,0:T(8,128)(2,1)S(1)}, bf16[1,256,1280]{2,1,0:T(8,128)(2,1)}, u32[]{:S(2)}) copy-start(bf16[1,256,1280]{2,1,0:T(8,128)(2,1)} %param.22) | copy-start | bytes 1966084
  6.5 38.4 %copy-start.12 = (bf16[1,1280,320]{1,2,0:T(8,128)(2,1)S(1)}, bf16[1,1280,320]{1,2,0:T(8,128)(2,1)}, u32[]{:S(2)}) copy-start(bf16[1,1280,320]{1,2,0:T(8,128)(2,1)} %param.26) | copy-start | bytes 2457604
  6.5 40.4 %copy-start.13 = (bf16[1,1280,320]{1,2,0:T(8,128)(2,1)S(1)}, bf16[1,1280,320]{1,2,0:T(8,128)(2,1)}, u32[]{:S(2)}) copy-start(bf16[1,1280,320]{1,2,0:T(8,128)(2,1)} %param.27) | copy-start | bytes 2457604
  6.5 153.8 %all-gather.5.cloned.1.call-start = ((), (), s32[]{:S(2)}) async-start(), calls=%async_computation.8 | async-start | bytes 6604800 | tf_op jit(solution)/shard_map/all_gather | solution.py:70
  8.2 204.3 %all-gather.3.cloned.1.call-start = ((), (), s32[]{:S(2)}) async-start(), calls=%async_computation.7 | async-start | bytes 3962880 | tf_op jit(solution)/shard_map/all_gather | solution.py:114
  23.0 28.1 %all-to-all-start.1 = ((s32[128,1,2]{2,1,0:T(1,128)}), s32[128,1,2]{2,1,0:T(1,128)S(1)}, u32[]{:S(2)}, u32[]{:S(2)}) async-start(s32[128,1,2]{2,1,0:T(1,128)} %copy.47), calls=%async_computation.1 | async-start | bytes 131072 | tf_op jit(solution)/shard_map/all_to_all | solution.py:129
  40.4 21.7 %copy-start.1 = (bf16[128,1280]{1,0:T(8,128)(2,1)S(1)}, bf16[128,1280]{1,0:T(8,128)(2,1)}, u32[]{:S(2)}) copy-start(bf16[128,1280]{1,0:T(8,128)(2,1)} %param.28) | copy-start | bytes 983044
  51.1 21.6 %all-to-all-start = ((s32[128,1,1]{2,1,0:T(1,128)}), s32[128,1,1]{2,1,0:T(1,128)S(1)}, u32[]{:S(2)}, u32[]{:S(2)}) async-start(s32[128,1,1]{2,1,0:T(1,128)} %copy.45), calls=%async_computation | async-start | bytes 131072 | tf_op jit(solution)/shard_map/all_to_all | solution.py:87
  63.4 16.3 %copy-start.27 = (s32[1,128]{1,0:T(1,128)S(1)}, s32[1,128]{1,0:T(1,128)}, u32[]{:S(2)}) copy-start(s32[1,128]{1,0:T(1,128)} %param.31) | copy-start | bytes 1540
  63.4 16.9 %copy-start.22 = (s32[128,1]{0,1:T(1,128)S(1)}, s32[128,1]{0,1:T(1,128)}, u32[]{:S(2)}) copy-start(s32[128,1]{0,1:T(1,128)} %param.19) | copy-start | bytes 1540
  63.4 43.5 %copy-start.18 = (bf16[320,10]{0,1:T(8,128)(2,1)S(1)}, bf16[320,10]{0,1:T(8,128)(2,1)}, u32[]{:S(2)}) copy-start(bf16[320,10]{0,1:T(8,128)(2,1)} %param.25) | copy-start | bytes 19204
  72.7 34.3 %all-to-all-start.2 = ((bf16[128,2,1280]{2,1,0:T(2,128)(2,1)}), bf16[128,2,1280]{2,1,0:T(2,128)(2,1)S(1)}, u32[]{:S(2)}, u32[]{:S(2)}) async-start(bf16[128,2,1280]{2,1,0:T(2,128)(2,1)} %reshape.356), calls=%async_computation.2 | async-start | bytes 1310720 | tf_op jit(solution)/shard_map/all_to_all | solution.py:130
  108.3 50.7 %all-to-all-start.4 = ((bf16[128,320,10]{1,2,0:T(8,128)(2,1)}), bf16[128,320,10]{1,2,0:T(8,128)(2,1)S(1)}, u32[]{:S(2)}, u32[]{:S(2)}) async-start(bf16[128,320,10]{1,2,0:T(8,128)(2,1)} %stack.2), calls=%async_computation.5 | async-start | bytes 3145728 | tf_op jit(solution)/shard_map/all_to_all | solution.py:150
  116.0 124.0 %reduce-scatter.3.cloned.1.call-start = ((), (), s32[]{:S(2)}) async-start(), calls=%async_computation.9 | async-start | bytes 819200 | tf_op jit(solution)/shard_map/reduce_scatter | solution.py:73
  123.0 37.4 %copy-start.16 = (bf16[128,1,1280]{2,0,1:T(8,128)(2,1)S(1)}, bf16[128,1,1280]{2,0,1:T(8,128)(2,1)}, u32[]{:S(2)}) copy-start(bf16[128,1,1280]{2,0,1:T(8,128)(2,1)} %param.16) | copy-start | bytes 983044
  123.0 37.4 %copy-start.26 = (f32[1280]{0:T(1024)S(1)}, f32[1280]{0:T(1024)}, u32[]{:S(2)}) copy-start(f32[1280]{0:T(1024)} %param.17) | copy-start | bytes 15364
  124.5 41.0 %copy-start.10 = (bf16[128,1280]{1,0:T(8,128)(2,1)}, bf16[128,1280]{1,0:T(8,128)(2,1)S(1)}, u32[]{:S(2)}) copy-start(bf16[128,1280]{1,0:T(8,128)(2,1)S(1)} %gather_fusion.1) | copy-start | bytes 983044
  124.5 35.9 %copy-start.29 = (f32[128]{0:T(128)S(1)}, f32[128]{0:T(128)}, u32[]{:S(2)}) copy-start(f32[128]{0:T(128)} %add_rsqrt_fusion.1) | copy-start | bytes 1540
  223.2 49.9 %copy-start.19 = (f32[1280]{0:T(1024)S(1)}, f32[1280]{0:T(1024)}, u32[]{:S(2)}) copy-start(f32[1280]{0:T(1024)} %param.23) | copy-start | bytes 15364
  223.2 49.9 %copy-start.30 = (f32[128]{0:T(128)S(1)}, f32[128]{0:T(128)}, u32[]{:S(2)}) copy-start(f32[128]{0:T(128)} %add_rsqrt_fusion.2) | copy-start | bytes 1540
  227.1 53.9 %copy-start.5 = (bf16[1,1280,320]{1,2,0:T(8,128)(2,1)}, bf16[1,1280,320]{1,2,0:T(8,128)(2,1)S(1)}, u32[]{:S(2)}) copy-start(bf16[1,1280,320]{1,2,0:T(8,128)(2,1)S(1)} %copy.64) | copy-start | bytes 2457604
  258.4 32.5 %all-to-all-start.3 = ((bf16[128,2,320]{2,1,0:T(2,128)(2,1)}), bf16[128,2,320]{2,1,0:T(2,128)(2,1)}, u32[]{:S(2)}, u32[]{:S(2)}) async-start(bf16[128,2,320]{2,1,0:T(2,128)(2,1)} %scatter_fusion.2), calls=%async_computation.4 | async-start | bytes 393216 | tf_op jit(solution)/shard_map/all_to_all | solution.py:86
  272.8 83.7 %reduce-scatter.5.cloned.1.call-start = ((), (), s32[]{:S(2)}) async-start(), calls=%async_computation.10 | async-start | bytes 1638400 | tf_op jit(solution)/shard_map/reduce_scatter | solution.py:154
  283.8 7.1 %copy-start.7 = (bf16[1,1280,320]{1,2,0:T(8,128)(2,1)}, bf16[1,1280,320]{1,2,0:T(8,128)(2,1)S(1)}, u32[]{:S(2)}) copy-start(bf16[1,1280,320]{1,2,0:T(8,128)(2,1)S(1)} %copy.62) | copy-start | bytes 2457604
  283.8 5.5 %copy-start.2 = (bf16[1,1280,320]{2,1,0:T(8,128)(2,1)S(1)}, bf16[1,1280,320]{2,1,0:T(8,128)(2,1)}, u32[]{:S(2)}) copy-start(bf16[1,1280,320]{2,1,0:T(8,128)(2,1)} %copy.46) | copy-start | bytes 2457604
  283.8 5.5 %copy-start.23 = (s32[128]{0:T(128)S(1)}, s32[128]{0:T(128)}, u32[]{:S(2)}) copy-start(s32[128]{0:T(128)} %fusion.49) | copy-start | bytes 1540
  285.7 20.2 %copy-start.9 = (bf16[256,1280]{1,0:T(8,128)(2,1)S(1)}, bf16[256,1280]{1,0:T(8,128)(2,1)}, u32[]{:S(2)}) copy-start(bf16[256,1280]{1,0:T(8,128)(2,1)} %gather_fusion.2) | copy-start | bytes 1966084
  289.3 16.7 %copy-start.20 = (s32[256]{0:T(256)S(1)}, s32[256]{0:T(256)}, u32[]{:S(2)}) copy-start(s32[256]{0:T(256)} %get-tuple-element.16) | copy-start | bytes 3076
  289.3 16.7 %copy-start.21 = (s32[256]{0:T(256)S(1)}, s32[256]{0:T(256)}, u32[]{:S(2)}) copy-start(s32[256]{0:T(256)} %get-tuple-element.17) | copy-start | bytes 3076
  289.3 16.7 %copy-start.24 = (pred[256]{0:T(512)(128)(4,1)S(1)}, pred[256]{0:T(512)(128)(4,1)}, u32[]{:S(2)}) copy-start(pred[256]{0:T(512)(128)(4,1)} %get-tuple-element.14) | copy-start | bytes 772
  289.3 16.7 %copy-start.25 = (pred[256]{0:T(512)(128)(4,1)S(1)}, pred[256]{0:T(512)(128)(4,1)}, u32[]{:S(2)}) copy-start(pred[256]{0:T(512)(128)(4,1)} %get-tuple-element.15) | copy-start | bytes 772
  305.9 1.1 copy-start.6
  306.5 1.7 copy-start.8
  306.5 3.8 %copy-start.3 = (bf16[1280,320]{1,0:T(8,128)(2,1)S(1)}, bf16[1280,320]{1,0:T(8,128)(2,1)}, u32[]{:S(2)}) copy-start(bf16[1280,320]{1,0:T(8,128)(2,1)} %scatter_fusion.3) | copy-start | bytes 2457604
  311.5 4.6 %copy-start.14 = (bf16[256,320]{0,1:T(8,128)(2,1)S(1)}, bf16[256,320]{0,1:T(8,128)(2,1)}, u32[]{:S(2)}) copy-start(bf16[256,320]{0,1:T(8,128)(2,1)} %convolution_convert_fusion.3) | copy-start | bytes 491524
  316.1 1.7 copy-start.15
  317.8 3.8 %copy-start.11 = (bf16[1536,320]{0,1:T(8,128)(2,1)S(1)}, bf16[1536,320]{0,1:T(8,128)(2,1)}, u32[]{:S(2)}) copy-start(bf16[1536,320]{0,1:T(8,128)(2,1)} %copy.60) | copy-start | bytes 2949124
  317.8 3.8 %copy-start.17 = (bf16[256,320]{0,1:T(8,128)(2,1)S(1)}, bf16[256,320]{0,1:T(8,128)(2,1)}, u32[]{:S(2)}) copy-start(bf16[256,320]{0,1:T(8,128)(2,1)} %convolution_convert_fusion.2) | copy-start | bytes 491524
  317.8 3.8 %copy-start.28 = (pred[256]{0:T(512)(128)(4,1)S(1)}, pred[256]{0:T(512)(128)(4,1)}, u32[]{:S(2)}) copy-start(pred[256]{0:T(512)(128)(4,1)} %iota_compare_fusion.4) | copy-start | bytes 772
  321.6 4.0 %copy-start.4 = (bf16[320,1280]{0,1:T(8,128)(2,1)S(1)}, bf16[320,1280]{0,1:T(8,128)(2,1)}, u32[]{:S(2)}) copy-start(bf16[320,1280]{0,1:T(8,128)(2,1)} %reshape.353) | copy-start | bytes 2457604
Sparse Core Ops, SparseCore 0:
  10.6 101.0 all-gather.4
  114.8 97.5 all-gather.2
  215.3 24.6 reduce-scatter.2
  327.3 29.2 reduce-scatter.4
